TPU v7x, 32 devices: a whole 2x2x4 slice. The times are simulated.
32 devices in a mesh: gen: 4 (over y, x), fit: 8 (over z, core).
Axes of the slice: x: 2, y: 2, z: 4, core: 2. Of those that a mesh axis runs over, the one named last changes fastest.
Arguments:
- raw_columns: bfloat16 [8, 2000, 2000], P(None, 'gen', 'fit'), as said below
- pivot_pairs: int32 [8], replicated, may hold values from 0 to 3999999, as said below
- collocation: bfloat16 [2000, 4096], P('gen', 'fit'), may hold values from -0.125 to 0.125
- metric_factor: float32 [4096, 4096], P('fit', 'gen'), as said below
Outputs:
- panel: float32 [8, 4096], P('gen', 'fit')
Inputs may be any that keep to these rules, and one draw needn't show every extreme that they name: `pivot_pairs`: 8 distinct orbital-pair indices p * 2000 + q. The entries at the pivots, raw_columns[P, pivot_pairs[Q] // 2000, pivot_pairs[Q] % 2000], form a symmetric positive definite matrix. `metric_factor`: lower triangular with a positive diagonal.
All inputs are finite; a program needn't handle non-finite values.
Results may differ from a plain program's by a relative error of at most 0.0029.
Values may be sent and summed in bfloat16 or wider, within the bound.
No kernel may reach another device: no remote copies, remote signals or barrier semaphores. Data moves between devices by JAX's collectives and lax.ppermute only.
A program may use at most 64 MiB of HBM per device.

v0:
```python
import math
import jax
import jax.numpy as jnp
from jax import lax
from jax.sharding import PartitionSpec as P

NORB = 2000


def spread(value, axis, source):
    kept = jnp.where(lax.axis_index(axis) == source, value, 0).astype(value.dtype)
    return lax.psum(kept, axis)


def project_block(vectors, stacked, orbital_count):
    point_count = stacked.shape[1]
    block_width = math.gcd(point_count, 512)
    block_count = point_count // block_width
    pair_count = stacked.shape[0] - orbital_count
    orbital_part = (
        stacked[:orbital_count].reshape(orbital_count, block_count, block_width).transpose(1, 0, 2)
    )
    pair_part = (
        stacked[orbital_count:].reshape(pair_count, block_count, block_width).transpose(1, 0, 2)
    )

    def one_block(pieces):
        mixed_terms = jnp.einsum(
            "apq,pn->aqn", vectors, pieces[0], preferred_element_type=jnp.float32
        )
        return jnp.sum(mixed_terms * pieces[1].astype(jnp.float32)[None], axis=1)

    blocks = lax.map(one_block, (orbital_part, pair_part))
    return blocks.transpose(1, 0, 2).reshape(vectors.shape[0], point_count)


def on_device(raw_columns, pivot_pairs, collocation, metric_factor):
    vec_total, orb_block, pair_block = raw_columns.shape
    gen_count = lax.axis_size("gen")
    fit_count = lax.axis_size("fit")
    gen_index = lax.axis_index("gen")
    fit_index = lax.axis_index("fit")
    point_dev = metric_factor.shape[0]
    vec_dev = vec_total // gen_count
    pair_first = pivot_pairs // NORB
    pair_second = pivot_pairs % NORB
    row_hits = (
        pair_first[:, None] == gen_index * orb_block + jnp.arange(orb_block)[None, :]
    ).astype(jnp.bfloat16)
    col_hits = (
        pair_second[:, None] == fit_index * pair_block + jnp.arange(pair_block)[None, :]
    ).astype(jnp.float32)
    picked = jnp.einsum("apq,bp->abq", raw_columns, row_hits, preferred_element_type=jnp.float32)
    own_entries = jnp.sum(picked * col_hits[None], axis=2)
    pivot_block = lax.psum(own_entries, ("gen", "fit"))
    factor = jnp.linalg.cholesky(pivot_block)
    flat_columns = raw_columns.reshape(vec_total, orb_block * pair_block).astype(jnp.float32)
    vectors = jax.scipy.linalg.solve_triangular(factor, flat_columns, lower=True)
    vectors = vectors.astype(jnp.bfloat16).reshape(vec_total, orb_block, pair_block)
    group_ratio = fit_count // gen_count
    owner_index = fit_index // group_ratio
    portion = fit_index % group_ratio
    orbital_side = lax.all_gather(collocation, "fit", axis=1, tiled=True)
    wide_slice = lax.dynamic_slice_in_dim(orbital_side, portion * pair_block, pair_block, 0)
    pair_side = spread(wide_slice, "gen", owner_index)
    partial_panel = project_block(
        vectors, jnp.concatenate([orbital_side, pair_side], axis=0), orb_block
    )
    arranged = partial_panel.reshape(gen_count, vec_dev, fit_count, point_dev).transpose(0, 2, 1, 3)
    arranged = arranged.reshape(gen_count * fit_count * vec_dev, point_dev)
    summed = lax.psum_scatter(arranged, ("gen", "fit"), scatter_dimension=0, tiled=True)
    remaining_start = jnp.zeros((vec_total, point_dev), jnp.float32)
    remaining_start = lax.dynamic_update_slice_in_dim(
        remaining_start, summed, gen_index * vec_dev, 0
    )

    def advance(turn_index, carried):
        remaining, solved = carried
        turn_owner = turn_index // group_ratio
        local_start = turn_index % group_ratio * point_dev
        whole_rest = lax.psum(remaining, "gen")
        column_part = lax.dynamic_slice_in_dim(metric_factor, local_start, point_dev, 1)
        candidate = jax.scipy.linalg.solve_triangular(column_part, whole_rest.T, lower=True).T
        holder = jnp.logical_and(fit_index == turn_index, gen_index == turn_owner)
        candidate = jnp.where(holder, candidate, 0.0)
        arrived = spread(candidate, ("gen", "fit"), turn_owner * fit_count + turn_index)
        update = jnp.dot(arrived, column_part.T, precision=lax.Precision.HIGHEST)
        remaining = remaining - jnp.where(gen_index == turn_owner, update, 0.0)
        own_rows = lax.dynamic_slice_in_dim(arrived, gen_index * vec_dev, vec_dev, 0)
        solved = jnp.where(fit_index == turn_index, own_rows, solved)
        return (remaining, solved)

    initial = jnp.zeros((vec_dev, point_dev), jnp.float32)
    remaining, solved = lax.fori_loop(0, fit_count, advance, (remaining_start, initial))
    return solved


def solution(mesh):
    in_specs = (P(None, "gen", "fit"), P(), P("gen", "fit"), P("fit", "gen"))
    out_specs = P("gen", "fit")
    return jax.shard_map(
        on_device, mesh=mesh, in_specs=in_specs, out_specs=out_specs, check_vma=False
    )
```

profile of v0, /device:TPU:0, one launch (start us, length us, event | category | flops | bytes accessed | tf_op | source)
XLA Modules:
  0.0 1175.4 jit_solution(14042528507513244858)
XLA Ops:
  7.3 50.9 %all-gather.2.cloned.1.call-done = bf16[500,4096]{1,0:T(8,128)(2,1)} async-done(((bf16[500,512]{1,0:T(8,128)(2,1)}), bf16[500,4096]{1,0:T(8,128)(2,1)}) %all-gather.2.cloned.1.call-update) | async-done | bytes 4096016 | tf_op jit(solution)/shard_map/all_gather | solution.py:63
  67.0 39.1 %psum.42 = f32[8,8]{0,1:T(8,128)S(1)} all-reduce(f32[8,8]{0,1:T(8,128)S(1)} %bitcast.108), channel_id=1, replica_groups=mesh['gen'=4,'fit'=8] {'gen','fit'}, use_global_device_ids=true, to_apply=%region_2.3 | all-reduce | flops 64 | bytes 512 | tf_op jit(solution)/shard_map/psum | solution.py:55
  108.8 7.2 reshape.130
  116.0 4.1 reshape.104
  123.1 4.2 reshape.132
  127.3 6.0 reshape.105
  133.3 6.5 copy.18
  139.8 6.5 copy.25
  146.3 35.0 %while.31 = (s32[]{:T(128)}, f32[8,8,512]{2,1,0:T(8,128)S(1)}, bf16[8,500,512]{2,1,0:T(8,128)(2,1)}, bf16[8,500,250]{2,1,0:T(8,128)(2,1)}, bf16[8,250,512]{1,2,0:T(8,128)(2,1)}, /*index=5*/s32[]{:T(128)}) while((s32[]{:T(128)}, f32[8,8,512]{2,1,0:T(8,128)S(1)}, bf16[8,500,512]{2,1,0:T(8,128)(2,1)}, bf16[8,500,250]{2,1,0:T(8,128)(2,1)}, ...), condition=%wide.region_7.8_spmd, body=%wide.region_5.7_spmd.sunk | while | flops 1026171904 | bytes 4934221 | solution.py:33
  156.3 3.1 fusion.70
  160.7 3.1 fusion.70
  165.0 3.1 fusion.70
  169.4 3.1 fusion.70
  178.1 3.1 fusion.70
  182.1 122.3 %all-reduce.6.cloned.1.call-done = f32[64,512]{1,0:T(8,128)} async-done(((f32[64,512]{1,0:T(8,128)}), f32[64,512]{1,0:T(8,128)}) %all-reduce.6.cloned.1.call-update) | async-done | bytes 131088
  305.2 863.1 %while.33 = (s32[]{:T(128)}, f32[8,512]{1,0:T(8,128)S(1)}, f32[2,512]{1,0:T(2,128)S(1)}, s32[]{:T(128)}, s32[]{:T(128)}, /*index=5*/f32[512,1024]{1,0:T(8,128)S(...) while((s32[]{:T(128)}, f32[8,512]{1,0:T(8,128)S(1)}, ...), condition=%wide.region_12.13_spmd.clone, body=%wide.region_9.12_spmd.clone.sunk | while | flops 41468964 | bytes 4176043 | solution.py:94
  305.6 10.0 while.34
  315.6 40.1 %custom-call.26 = f32[4,128,128]{1,2,0:T(8,128)S(1)} custom-call(f32[4,128,128]{2,1,0:T(8,128)} %get-tuple-element.386), custom_call_target="InvertDiagBlocksLowerTriangular" | custom-call | tf_op jit(solution)/shard_map/while/body/eval_jaxpr/jit(_solve_triangular)/triangular_solve | solution.py:83
  355.7 15.9 %psum.48 = f32[512,8]{0,1:T(8,128)S(1)} all-reduce(f32[512,8]{0,1:T(8,128)S(1)} %bitcast.105), channel_id=1, replica_groups=mesh['gen'=4,'fit'=8] {'gen'}, use_global_device_ids=true, to_apply=%region_10.10 | all-reduce | flops 4096 | bytes 32768 | tf_op jit(solution)/shard_map/while/body/eval_jaxpr/psum | solution.py:81
  373.1 38.4 %psum.49 = f32[8,512]{1,0:T(8,128)S(1)} all-reduce(f32[8,512]{1,0:T(8,128)S(1)} %fusion.88), channel_id=1, replica_groups=mesh['gen'=4,'fit'=8] {'gen','fit'}, use_global_device_ids=true, to_apply=%region_11.11 | all-reduce | flops 4096 | bytes 32768 | tf_op jit(solution)/shard_map/while/body/eval_jaxpr/psum | solution.py:12
  412.7 10.0 while.34
  422.8 40.1 %custom-call.26 = f32[4,128,128]{1,2,0:T(8,128)S(1)} custom-call(f32[4,128,128]{2,1,0:T(8,128)} %get-tuple-element.386), custom_call_target="InvertDiagBlocksLowerTriangular" | custom-call | tf_op jit(solution)/shard_map/while/body/eval_jaxpr/jit(_solve_triangular)/triangular_solve | solution.py:83
  462.9 16.7 %psum.48 = f32[512,8]{0,1:T(8,128)S(1)} all-reduce(f32[512,8]{0,1:T(8,128)S(1)} %bitcast.105), channel_id=1, replica_groups=mesh['gen'=4,'fit'=8] {'gen'}, use_global_device_ids=true, to_apply=%region_10.10 | all-reduce | flops 4096 | bytes 32768 | tf_op jit(solution)/shard_map/while/body/eval_jaxpr/psum | solution.py:81
  481.1 38.4 %psum.49 = f32[8,512]{1,0:T(8,128)S(1)} all-reduce(f32[8,512]{1,0:T(8,128)S(1)} %fusion.88), channel_id=1, replica_groups=mesh['gen'=4,'fit'=8] {'gen','fit'}, use_global_device_ids=true, to_apply=%region_11.11 | all-reduce | flops 4096 | bytes 32768 | tf_op jit(solution)/shard_map/while/body/eval_jaxpr/psum | solution.py:12
  520.7 10.0 while.34
  530.7 40.1 %custom-call.26 = f32[4,128,128]{1,2,0:T(8,128)S(1)} custom-call(f32[4,128,128]{2,1,0:T(8,128)} %get-tuple-element.386), custom_call_target="InvertDiagBlocksLowerTriangular" | custom-call | tf_op jit(solution)/shard_map/while/body/eval_jaxpr/jit(_solve_triangular)/triangular_solve | solution.py:83
  570.9 16.7 %psum.48 = f32[512,8]{0,1:T(8,128)S(1)} all-reduce(f32[512,8]{0,1:T(8,128)S(1)} %bitcast.105), channel_id=1, replica_groups=mesh['gen'=4,'fit'=8] {'gen'}, use_global_device_ids=true, to_apply=%region_10.10 | all-reduce | flops 4096 | bytes 32768 | tf_op jit(solution)/shard_map/while/body/eval_jaxpr/psum | solution.py:81
  589.1 38.4 %psum.49 = f32[8,512]{1,0:T(8,128)S(1)} all-reduce(f32[8,512]{1,0:T(8,128)S(1)} %fusion.88), channel_id=1, replica_groups=mesh['gen'=4,'fit'=8] {'gen','fit'}, use_global_device_ids=true, to_apply=%region_11.11 | all-reduce | flops 4096 | bytes 32768 | tf_op jit(solution)/shard_map/while/body/eval_jaxpr/psum | solution.py:12
  628.7 10.0 while.34
  638.7 40.1 %custom-call.26 = f32[4,128,128]{1,2,0:T(8,128)S(1)} custom-call(f32[4,128,128]{2,1,0:T(8,128)} %get-tuple-element.386), custom_call_target="InvertDiagBlocksLowerTriangular" | custom-call | tf_op jit(solution)/shard_map/while/body/eval_jaxpr/jit(_solve_triangular)/triangular_solve | solution.py:83
  678.8 16.7 %psum.48 = f32[512,8]{0,1:T(8,128)S(1)} all-reduce(f32[512,8]{0,1:T(8,128)S(1)} %bitcast.105), channel_id=1, replica_groups=mesh['gen'=4,'fit'=8] {'gen'}, use_global_device_ids=true, to_apply=%region_10.10 | all-reduce | flops 4096 | bytes 32768 | tf_op jit(solution)/shard_map/while/body/eval_jaxpr/psum | solution.py:81
  697.0 38.4 %psum.49 = f32[8,512]{1,0:T(8,128)S(1)} all-reduce(f32[8,512]{1,0:T(8,128)S(1)} %fusion.88), channel_id=1, replica_groups=mesh['gen'=4,'fit'=8] {'gen','fit'}, use_global_device_ids=true, to_apply=%region_11.11 | all-reduce | flops 4096 | bytes 32768 | tf_op jit(solution)/shard_map/while/body/eval_jaxpr/psum | solution.py:12
  736.6 10.0 while.34
  746.7 40.1 %custom-call.26 = f32[4,128,128]{1,2,0:T(8,128)S(1)} custom-call(f32[4,128,128]{2,1,0:T(8,128)} %get-tuple-element.386), custom_call_target="InvertDiagBlocksLowerTriangular" | custom-call | tf_op jit(solution)/shard_map/while/body/eval_jaxpr/jit(_solve_triangular)/triangular_solve | solution.py:83
  786.8 16.7 %psum.48 = f32[512,8]{0,1:T(8,128)S(1)} all-reduce(f32[512,8]{0,1:T(8,128)S(1)} %bitcast.105), channel_id=1, replica_groups=mesh['gen'=4,'fit'=8] {'gen'}, use_global_device_ids=true, to_apply=%region_10.10 | all-reduce | flops 4096 | bytes 32768 | tf_op jit(solution)/shard_map/while/body/eval_jaxpr/psum | solution.py:81
  805.0 38.4 %psum.49 = f32[8,512]{1,0:T(8,128)S(1)} all-reduce(f32[8,512]{1,0:T(8,128)S(1)} %fusion.88), channel_id=1, replica_groups=mesh['gen'=4,'fit'=8] {'gen','fit'}, use_global_device_ids=true, to_apply=%region_11.11 | all-reduce | flops 4096 | bytes 32768 | tf_op jit(solution)/shard_map/while/body/eval_jaxpr/psum | solution.py:12
  844.6 10.0 while.34
  854.6 40.1 %custom-call.26 = f32[4,128,128]{1,2,0:T(8,128)S(1)} custom-call(f32[4,128,128]{2,1,0:T(8,128)} %get-tuple-element.386), custom_call_target="InvertDiagBlocksLowerTriangular" | custom-call | tf_op jit(solution)/shard_map/while/body/eval_jaxpr/jit(_solve_triangular)/triangular_solve | solution.py:83
  894.8 16.8 %psum.48 = f32[512,8]{0,1:T(8,128)S(1)} all-reduce(f32[512,8]{0,1:T(8,128)S(1)} %bitcast.105), channel_id=1, replica_groups=mesh['gen'=4,'fit'=8] {'gen'}, use_global_device_ids=true, to_apply=%region_10.10 | all-reduce | flops 4096 | bytes 32768 | tf_op jit(solution)/shard_map/while/body/eval_jaxpr/psum | solution.py:81
  913.0 38.4 %psum.49 = f32[8,512]{1,0:T(8,128)S(1)} all-reduce(f32[8,512]{1,0:T(8,128)S(1)} %fusion.88), channel_id=1, replica_groups=mesh['gen'=4,'fit'=8] {'gen','fit'}, use_global_device_ids=true, to_apply=%region_11.11 | all-reduce | flops 4096 | bytes 32768 | tf_op jit(solution)/shard_map/while/body/eval_jaxpr/psum | solution.py:12
  952.5 10.0 while.34
  962.6 40.1 %custom-call.26 = f32[4,128,128]{1,2,0:T(8,128)S(1)} custom-call(f32[4,128,128]{2,1,0:T(8,128)} %get-tuple-element.386), custom_call_target="InvertDiagBlocksLowerTriangular" | custom-call | tf_op jit(solution)/shard_map/while/body/eval_jaxpr/jit(_solve_triangular)/triangular_solve | solution.py:83
  1002.7 16.8 %psum.48 = f32[512,8]{0,1:T(8,128)S(1)} all-reduce(f32[512,8]{0,1:T(8,128)S(1)} %bitcast.105), channel_id=1, replica_groups=mesh['gen'=4,'fit'=8] {'gen'}, use_global_device_ids=true, to_apply=%region_10.10 | all-reduce | flops 4096 | bytes 32768 | tf_op jit(solution)/shard_map/while/body/eval_jaxpr/psum | solution.py:81
  1020.9 38.4 %psum.49 = f32[8,512]{1,0:T(8,128)S(1)} all-reduce(f32[8,512]{1,0:T(8,128)S(1)} %fusion.88), channel_id=1, replica_groups=mesh['gen'=4,'fit'=8] {'gen','fit'}, use_global_device_ids=true, to_apply=%region_11.11 | all-reduce | flops 4096 | bytes 32768 | tf_op jit(solution)/shard_map/while/body/eval_jaxpr/psum | solution.py:12
  1060.5 10.0 while.34
  1070.6 40.1 %custom-call.26 = f32[4,128,128]{1,2,0:T(8,128)S(1)} custom-call(f32[4,128,128]{2,1,0:T(8,128)} %get-tuple-element.386), custom_call_target="InvertDiagBlocksLowerTriangular" | custom-call | tf_op jit(solution)/shard_map/while/body/eval_jaxpr/jit(_solve_triangular)/triangular_solve | solution.py:83
  1110.7 16.8 %psum.48 = f32[512,8]{0,1:T(8,128)S(1)} all-reduce(f32[512,8]{0,1:T(8,128)S(1)} %bitcast.105), channel_id=1, replica_groups=mesh['gen'=4,'fit'=8] {'gen'}, use_global_device_ids=true, to_apply=%region_10.10 | all-reduce | flops 4096 | bytes 32768 | tf_op jit(solution)/shard_map/while/body/eval_jaxpr/psum | solution.py:81
  1128.9 38.4 %psum.49 = f32[8,512]{1,0:T(8,128)S(1)} all-reduce(f32[8,512]{1,0:T(8,128)S(1)} %fusion.88), channel_id=1, replica_groups=mesh['gen'=4,'fit'=8] {'gen','fit'}, use_global_device_ids=true, to_apply=%region_11.11 | all-reduce | flops 4096 | bytes 32768 | tf_op jit(solution)/shard_map/while/body/eval_jaxpr/psum | solution.py:12
  (282 shorter events, 136.9 us)
Async XLA Ops:
  6.5 51.7 %all-gather.2.cloned.1.call-start = ((), (), s32[]{:S(2)}) async-start(), calls=%async_computation | async-start | bytes 4644864 | tf_op jit(solution)/shard_map/all_gather | solution.py:63
  7.3 139.0 %all-reduce.4.cloned.1.call-start = ((), (), s32[]{:S(2)}) async-start(), calls=%async_computation.1 | async-start | bytes 4194304 | tf_op jit(solution)/shard_map/psum | solution.py:12
  62.9 1.6 copy-start.1
  63.0 3.3 copy-start.3
  63.0 241.5 %all-reduce.6.cloned.1.call-start = ((), (), s32[]{:S(2)}) async-start(), calls=%async_computation.2 | async-start | bytes 262144
  146.3 158.9 %copy-start = (f32[512,1024]{1,0:T(8,128)S(1)}, f32[512,1024]{1,0:T(8,128)}, u32[]{:S(2)}) copy-start(f32[512,1024]{1,0:T(8,128)} %param.11) | copy-start | bytes 6291460
  1168.3 0.6 copy-start.2
Sparse Core Ops, SparseCore 0:
  9.0 49.1 all-gather.1
  63.1 69.2 all-reduce.3
  182.2 122.1 all-reduce.5
where the time goes:
time: 1180 us
  blocking collectives  480 us (41%)
  other arithmetic  328 us (28%)
  waiting for transfers between devices  174 us (15%)
  local copies, waits for them, and re-layouts  132 us (11%)
  matrix products  47.8 us (4%)
  between operations  13.3 us (1%)
    another operation x24, other arithmetic, advance(): jax.scipy.linalg.solve_triangular(column_part, whole_rest.T, lower=True)  322 us
    psum x8, blocking collectives, spread(): return lax.psum(kept, axis)  307 us
    psum x8, blocking collectives, advance(): whole_rest = lax.psum(remaining, 'gen')  133 us
    unnamed x4, waiting for transfers between devices  123 us
    another operation x96, local copies, waits for them, and re-layouts  80.2 us
    all_gather x1, waiting for transfers between devices, on_device(): orbital_side = lax.all_gather(collocation, 'fit', axis=1, tiled=True)  50.9 us
    psum x1, blocking collectives, on_device(): pivot_block = lax.psum(own_entries, ('gen', 'fit'))  39.1 us
    dot_general x8, matrix products, one_block(): jnp.einsum('apq,pn->aqn', vectors, pieces[0], preferred_element_type=jnp....  25.1 us
  transfers between devices with their start and end apart: 3, of which 2 were waited for; matrix products, arithmetic and copies ran while one was open for 4% of the time, Pallas kernels for 0%

commit v1 on v0

--- a/solution.py
+++ b/solution.py
@@ -5,6 +5,18 @@
 from jax.sharding import PartitionSpec as P
 
 NORB = 2000
+
+
+def doubled_up(array, axis, dim):
+    ways, here = (lax.axis_size(axis), lax.axis_index(axis))
+    grown, reach = (array, 1)
+    while reach < ways:
+        theirs = lax.ppermute(grown, axis, [(d, d ^ reach) for d in range(ways)])
+        mine_first = jnp.concatenate([grown, theirs], axis=dim)
+        theirs_first = jnp.concatenate([theirs, grown], axis=dim)
+        grown = jnp.where(here & reach == 0, mine_first, theirs_first)
+        reach = 2 * reach
+    return grown
 
 
 def spread(value, axis, source):
@@ -60,7 +72,7 @@
     group_ratio = fit_count // gen_count
     owner_index = fit_index // group_ratio
     portion = fit_index % group_ratio
-    orbital_side = lax.all_gather(collocation, "fit", axis=1, tiled=True)
+    orbital_side = doubled_up(collocation, "fit", 1)
     wide_slice = lax.dynamic_slice_in_dim(orbital_side, portion * pair_block, pair_block, 0)
     pair_side = spread(wide_slice, "gen", owner_index)
     partial_panel = project_block(

time: 1180 us -> 1260 us (1.068)
  waiting for transfers between devices: 174 us -> 237 us
    ppermute x0 -> x3, waiting for transfers between devices: none -> 114 us  [doubled_up(): theirs = lax.ppermute(grown, axis, [(d, d ^ reach) for d in range(ways)])]
    all_gather x1 -> x0, waiting for transfers between devices: 50.9 us -> none  [on_device(): orbital_side = lax.all_gather(collocation, 'fit', axis=1, tiled=True)]
    unnamed x4 -> x3, waiting for transfers between devices: 123 us -> 123 us
  transfers between devices with their start and end apart: 3 -> 5, of which waited for: 2 -> 4; matrix products, arithmetic and copies ran while one was open for 4% -> 3% of each run, Pallas kernels for 0% -> 0%
where the time goes in v1:
time: 1260 us
  blocking collectives  481 us (38%)
  other arithmetic  339 us (27%)
  waiting for transfers between devices  237 us (19%)
  local copies, waits for them, and re-layouts  133 us (11%)
  matrix products  47.8 us (4%)
  between operations  13.6 us (1%)
    another operation x24, other arithmetic, advance(): jax.scipy.linalg.solve_triangular(column_part, whole_rest.T, lower=True)  322 us
    psum x8, blocking collectives, spread(): return lax.psum(kept, axis)  307 us
    psum x8, blocking collectives, advance(): whole_rest = lax.psum(remaining, 'gen')  133 us
    unnamed x3, waiting for transfers between devices  123 us
    ppermute x3, waiting for transfers between devices, doubled_up(): theirs = lax.ppermute(grown, axis, [(d, d ^ reach) for d in range(ways)])  114 us
    another operation x96, local copies, waits for them, and re-layouts  80.2 us
    psum x1, blocking collectives, on_device(): pivot_block = lax.psum(own_entries, ('gen', 'fit'))  40.1 us
  transfers between devices with their start and end apart: 5, of which 4 were waited for; matrix products, arithmetic and copies ran while one was open for 3% of the time, Pallas kernels for 0%

profile of v1, /device:TPU:0, one launch (start us, length us, event | category | flops | bytes accessed | tf_op | source)
XLA Modules:
  0.0 1259.3 jit_solution(13052507777995914292)
XLA Ops:
  14.6 23.3 %collective-permute-done.1 = bf16[500,1024]{1,0:T(8,128)(2,1)S(1)} collective-permute-done((bf16[500,1024]{1,0:T(8,128)(2,1)}, bf16[500,1024]{1,0:T(8,128)(2,1)S(1)}, u32[]{:S(2)}, u32[]{:S(2)}) %collective-permute-start.1) | collective-permute-done | bytes 1024032 | tf_op jit(solution)/shard_map/ppermute | solution.py:14
  46.0 89.1 %collective-permute-done.2 = bf16[500,2048]{1,0:T(8,128)(2,1)} collective-permute-done((bf16[500,2048]{1,0:T(8,128)(2,1)}, bf16[500,2048]{1,0:T(8,128)(2,1)}, u32[]{:S(2)}, u32[]{:S(2)}) %collective-permute-start.2) | collective-permute-done | bytes 2048032 | tf_op jit(solution)/shard_map/ppermute | solution.py:14
  135.1 3.9 copy.29
  139.0 6.4 fusion.31
  149.3 40.1 %psum.42 = f32[8,8]{0,1:T(8,128)S(1)} all-reduce(f32[8,8]{0,1:T(8,128)S(1)} %bitcast.114), channel_id=1, replica_groups=mesh['gen'=4,'fit'=8] {'gen','fit'}, use_global_device_ids=true, to_apply=%region_2.3 | all-reduce | flops 64 | bytes 512 | tf_op jit(solution)/shard_map/psum | solution.py:67
  192.2 7.3 reshape.139
  199.5 4.0 reshape.113
  206.5 4.2 reshape.141
  210.8 6.0 reshape.114
  222.6 6.5 copy.37
  229.1 35.0 %while.31 = (s32[]{:T(128)}, f32[8,8,512]{2,1,0:T(8,128)S(1)}, bf16[8,500,512]{2,1,0:T(8,128)(2,1)}, bf16[8,500,250]{2,1,0:T(8,128)(2,1)}, bf16[8,250,512]{1,2,0:T(8,128)(2,1)}, /*index=5*/s32[]{:T(128)}) while((s32[]{:T(128)}, f32[8,8,512]{2,1,0:T(8,128)S(1)}, bf16[8,500,512]{2,1,0:T(8,128)(2,1)}, bf16[8,500,250]{2,1,0:T(8,128)(2,1)}, ...), condition=%wide.region_7.8_spmd, body=%wide.region_5.7_spmd.sunk | while | flops 1026171904 | bytes 4934221 | solution.py:45
  230.5 3.1 fusion.75
  239.2 3.1 fusion.75
  243.5 3.1 fusion.75
  265.0 123.0 %all-reduce.6.cloned.1.call-done = f32[64,512]{1,0:T(8,128)} async-done(((f32[64,512]{1,0:T(8,128)}), f32[64,512]{1,0:T(8,128)}) %all-reduce.6.cloned.1.call-update) | async-done | bytes 131088
  388.7 863.1 %while.33 = (s32[]{:T(128)}, f32[8,512]{1,0:T(8,128)S(1)}, f32[2,512]{1,0:T(2,128)S(1)}, s32[]{:T(128)}, s32[]{:T(128)}, /*index=5*/f32[512,1024]{1,0:T(8,128)S(...) while((s32[]{:T(128)}, f32[8,512]{1,0:T(8,128)S(1)}, ...), condition=%wide.region_12.13_spmd.clone, body=%wide.region_9.12_spmd.clone.sunk | while | flops 41468964 | bytes 4176043 | solution.py:106
  389.1 10.0 while.34
  399.2 40.1 %custom-call.26 = f32[4,128,128]{1,2,0:T(8,128)S(1)} custom-call(f32[4,128,128]{2,1,0:T(8,128)} %get-tuple-element.386), custom_call_target="InvertDiagBlocksLowerTriangular" | custom-call | tf_op jit(solution)/shard_map/while/body/eval_jaxpr/jit(_solve_triangular)/triangular_solve | solution.py:95
  439.3 15.9 %psum.48 = f32[512,8]{0,1:T(8,128)S(1)} all-reduce(f32[512,8]{0,1:T(8,128)S(1)} %bitcast.111), channel_id=1, replica_groups=mesh['gen'=4,'fit'=8] {'gen'}, use_global_device_ids=true, to_apply=%region_10.10 | all-reduce | flops 4096 | bytes 32768 | tf_op jit(solution)/shard_map/while/body/eval_jaxpr/psum | solution.py:93
  456.7 38.4 %psum.49 = f32[8,512]{1,0:T(8,128)S(1)} all-reduce(f32[8,512]{1,0:T(8,128)S(1)} %fusion.93), channel_id=1, replica_groups=mesh['gen'=4,'fit'=8] {'gen','fit'}, use_global_device_ids=true, to_apply=%region_11.11 | all-reduce | flops 4096 | bytes 32768 | tf_op jit(solution)/shard_map/while/body/eval_jaxpr/psum | solution.py:24
  496.3 10.0 while.34
  506.3 40.1 %custom-call.26 = f32[4,128,128]{1,2,0:T(8,128)S(1)} custom-call(f32[4,128,128]{2,1,0:T(8,128)} %get-tuple-element.386), custom_call_target="InvertDiagBlocksLowerTriangular" | custom-call | tf_op jit(solution)/shard_map/while/body/eval_jaxpr/jit(_solve_triangular)/triangular_solve | solution.py:95
  546.5 16.7 %psum.48 = f32[512,8]{0,1:T(8,128)S(1)} all-reduce(f32[512,8]{0,1:T(8,128)S(1)} %bitcast.111), channel_id=1, replica_groups=mesh['gen'=4,'fit'=8] {'gen'}, use_global_device_ids=true, to_apply=%region_10.10 | all-reduce | flops 4096 | bytes 32768 | tf_op jit(solution)/shard_map/while/body/eval_jaxpr/psum | solution.py:93
  564.7 38.4 %psum.49 = f32[8,512]{1,0:T(8,128)S(1)} all-reduce(f32[8,512]{1,0:T(8,128)S(1)} %fusion.93), channel_id=1, replica_groups=mesh['gen'=4,'fit'=8] {'gen','fit'}, use_global_device_ids=true, to_apply=%region_11.11 | all-reduce | flops 4096 | bytes 32768 | tf_op jit(solution)/shard_map/while/body/eval_jaxpr/psum | solution.py:24
  604.3 10.0 while.34
  614.3 40.1 %custom-call.26 = f32[4,128,128]{1,2,0:T(8,128)S(1)} custom-call(f32[4,128,128]{2,1,0:T(8,128)} %get-tuple-element.386), custom_call_target="InvertDiagBlocksLowerTriangular" | custom-call | tf_op jit(solution)/shard_map/while/body/eval_jaxpr/jit(_solve_triangular)/triangular_solve | solution.py:95
  654.4 16.7 %psum.48 = f32[512,8]{0,1:T(8,128)S(1)} all-reduce(f32[512,8]{0,1:T(8,128)S(1)} %bitcast.111), channel_id=1, replica_groups=mesh['gen'=4,'fit'=8] {'gen'}, use_global_device_ids=true, to_apply=%region_10.10 | all-reduce | flops 4096 | bytes 32768 | tf_op jit(solution)/shard_map/while/body/eval_jaxpr/psum | solution.py:93
  672.6 38.4 %psum.49 = f32[8,512]{1,0:T(8,128)S(1)} all-reduce(f32[8,512]{1,0:T(8,128)S(1)} %fusion.93), channel_id=1, replica_groups=mesh['gen'=4,'fit'=8] {'gen','fit'}, use_global_device_ids=true, to_apply=%region_11.11 | all-reduce | flops 4096 | bytes 32768 | tf_op jit(solution)/shard_map/while/body/eval_jaxpr/psum | solution.py:24
  712.2 10.0 while.34
  722.3 40.1 %custom-call.26 = f32[4,128,128]{1,2,0:T(8,128)S(1)} custom-call(f32[4,128,128]{2,1,0:T(8,128)} %get-tuple-element.386), custom_call_target="InvertDiagBlocksLowerTriangular" | custom-call | tf_op jit(solution)/shard_map/while/body/eval_jaxpr/jit(_solve_triangular)/triangular_solve | solution.py:95
  762.4 16.7 %psum.48 = f32[512,8]{0,1:T(8,128)S(1)} all-reduce(f32[512,8]{0,1:T(8,128)S(1)} %bitcast.111), channel_id=1, replica_groups=mesh['gen'=4,'fit'=8] {'gen'}, use_global_device_ids=true, to_apply=%region_10.10 | all-reduce | flops 4096 | bytes 32768 | tf_op jit(solution)/shard_map/while/body/eval_jaxpr/psum | solution.py:93
  780.6 38.4 %psum.49 = f32[8,512]{1,0:T(8,128)S(1)} all-reduce(f32[8,512]{1,0:T(8,128)S(1)} %fusion.93), channel_id=1, replica_groups=mesh['gen'=4,'fit'=8] {'gen','fit'}, use_global_device_ids=true, to_apply=%region_11.11 | all-reduce | flops 4096 | bytes 32768 | tf_op jit(solution)/shard_map/while/body/eval_jaxpr/psum | solution.py:24
  820.2 10.0 while.34
  830.2 40.1 %custom-call.26 = f32[4,128,128]{1,2,0:T(8,128)S(1)} custom-call(f32[4,128,128]{2,1,0:T(8,128)} %get-tuple-element.386), custom_call_target="InvertDiagBlocksLowerTriangular" | custom-call | tf_op jit(solution)/shard_map/while/body/eval_jaxpr/jit(_solve_triangular)/triangular_solve | solution.py:95
  870.3 16.7 %psum.48 = f32[512,8]{0,1:T(8,128)S(1)} all-reduce(f32[512,8]{0,1:T(8,128)S(1)} %bitcast.111), channel_id=1, replica_groups=mesh['gen'=4,'fit'=8] {'gen'}, use_global_device_ids=true, to_apply=%region_10.10 | all-reduce | flops 4096 | bytes 32768 | tf_op jit(solution)/shard_map/while/body/eval_jaxpr/psum | solution.py:93
  888.5 38.4 %psum.49 = f32[8,512]{1,0:T(8,128)S(1)} all-reduce(f32[8,512]{1,0:T(8,128)S(1)} %fusion.93), channel_id=1, replica_groups=mesh['gen'=4,'fit'=8] {'gen','fit'}, use_global_device_ids=true, to_apply=%region_11.11 | all-reduce | flops 4096 | bytes 32768 | tf_op jit(solution)/shard_map/while/body/eval_jaxpr/psum | solution.py:24
  928.1 10.0 while.34
  938.2 40.1 %custom-call.26 = f32[4,128,128]{1,2,0:T(8,128)S(1)} custom-call(f32[4,128,128]{2,1,0:T(8,128)} %get-tuple-element.386), custom_call_target="InvertDiagBlocksLowerTriangular" | custom-call | tf_op jit(solution)/shard_map/while/body/eval_jaxpr/jit(_solve_triangular)/triangular_solve | solution.py:95
  978.3 16.8 %psum.48 = f32[512,8]{0,1:T(8,128)S(1)} all-reduce(f32[512,8]{0,1:T(8,128)S(1)} %bitcast.111), channel_id=1, replica_groups=mesh['gen'=4,'fit'=8] {'gen'}, use_global_device_ids=true, to_apply=%region_10.10 | all-reduce | flops 4096 | bytes 32768 | tf_op jit(solution)/shard_map/while/body/eval_jaxpr/psum | solution.py:93
  996.5 38.4 %psum.49 = f32[8,512]{1,0:T(8,128)S(1)} all-reduce(f32[8,512]{1,0:T(8,128)S(1)} %fusion.93), channel_id=1, replica_groups=mesh['gen'=4,'fit'=8] {'gen','fit'}, use_global_device_ids=true, to_apply=%region_11.11 | all-reduce | flops 4096 | bytes 32768 | tf_op jit(solution)/shard_map/while/body/eval_jaxpr/psum | solution.py:24
  1036.1 10.0 while.34
  1046.1 40.1 %custom-call.26 = f32[4,128,128]{1,2,0:T(8,128)S(1)} custom-call(f32[4,128,128]{2,1,0:T(8,128)} %get-tuple-element.386), custom_call_target="InvertDiagBlocksLowerTriangular" | custom-call | tf_op jit(solution)/shard_map/while/body/eval_jaxpr/jit(_solve_triangular)/triangular_solve | solution.py:95
  1086.3 16.8 %psum.48 = f32[512,8]{0,1:T(8,128)S(1)} all-reduce(f32[512,8]{0,1:T(8,128)S(1)} %bitcast.111), channel_id=1, replica_groups=mesh['gen'=4,'fit'=8] {'gen'}, use_global_device_ids=true, to_apply=%region_10.10 | all-reduce | flops 4096 | bytes 32768 | tf_op jit(solution)/shard_map/while/body/eval_jaxpr/psum | solution.py:93
  1104.5 38.4 %psum.49 = f32[8,512]{1,0:T(8,128)S(1)} all-reduce(f32[8,512]{1,0:T(8,128)S(1)} %fusion.93), channel_id=1, replica_groups=mesh['gen'=4,'fit'=8] {'gen','fit'}, use_global_device_ids=true, to_apply=%region_11.11 | all-reduce | flops 4096 | bytes 32768 | tf_op jit(solution)/shard_map/while/body/eval_jaxpr/psum | solution.py:24
  1144.0 10.0 while.34
  1154.1 40.1 %custom-call.26 = f32[4,128,128]{1,2,0:T(8,128)S(1)} custom-call(f32[4,128,128]{2,1,0:T(8,128)} %get-tuple-element.386), custom_call_target="InvertDiagBlocksLowerTriangular" | custom-call | tf_op jit(solution)/shard_map/while/body/eval_jaxpr/jit(_solve_triangular)/triangular_solve | solution.py:95
  1194.2 16.8 %psum.48 = f32[512,8]{0,1:T(8,128)S(1)} all-reduce(f32[512,8]{0,1:T(8,128)S(1)} %bitcast.111), channel_id=1, replica_groups=mesh['gen'=4,'fit'=8] {'gen'}, use_global_device_ids=true, to_apply=%region_10.10 | all-reduce | flops 4096 | bytes 32768 | tf_op jit(solution)/shard_map/while/body/eval_jaxpr/psum | solution.py:93
  1212.4 38.4 %psum.49 = f32[8,512]{1,0:T(8,128)S(1)} all-reduce(f32[8,512]{1,0:T(8,128)S(1)} %fusion.93), channel_id=1, replica_groups=mesh['gen'=4,'fit'=8] {'gen','fit'}, use_global_device_ids=true, to_apply=%region_11.11 | all-reduce | flops 4096 | bytes 32768 | tf_op jit(solution)/shard_map/while/body/eval_jaxpr/psum | solution.py:24
  (301 shorter events, 159.7 us)
Async XLA Ops:
  6.5 222.6 %all-reduce.4.cloned.1.call-start = ((), (), s32[]{:S(2)}) async-start(), calls=%async_computation | async-start | bytes 4194304 | tf_op jit(solution)/shard_map/psum | solution.py:24
  7.8 30.2 %copy-start.4 = (bf16[500,512]{0,1:T(8,128)(2,1)}, bf16[500,512]{0,1:T(8,128)(2,1)S(1)}, u32[]{:S(2)}) copy-start(bf16[500,512]{0,1:T(8,128)(2,1)S(1)} %copy.20) | copy-start | bytes 1536004
  7.8 2.1 collective-permute-start
  9.9 28.1 %copy-start.5 = (bf16[500,512]{0,1:T(8,128)(2,1)}, bf16[500,512]{0,1:T(8,128)(2,1)S(1)}, u32[]{:S(2)}) copy-start(bf16[500,512]{0,1:T(8,128)(2,1)S(1)} %collective-permute-done) | copy-start | bytes 1536004
  10.3 4.4 copy-start.2
  11.7 26.3 %collective-permute-start.1 = (bf16[500,1024]{1,0:T(8,128)(2,1)}, bf16[500,1024]{1,0:T(8,128)(2,1)S(1)}, u32[]{:S(2)}, u32[]{:S(2)}) collective-permute-start(bf16[500,1024]{1,0:T(8,128)(2,1)} %copy.24), channel_id=1, source_target_pairs={{0,2},{1,3},{2,0},{3,1},{4,6},{5,7},{6,4},{7,5},{8,10},{9,11},{10,... | collective-permute-start | bytes 3072008 | tf_op jit(solution)/shard_map/ppermute | solution.py:14
  40.7 5.3 copy-start.7
  43.2 91.9 %collective-permute-start.2 = (bf16[500,2048]{1,0:T(8,128)(2,1)}, bf16[500,2048]{1,0:T(8,128)(2,1)}, u32[]{:S(2)}, u32[]{:S(2)}) collective-permute-start(bf16[500,2048]{1,0:T(8,128)(2,1)} %copy.28), channel_id=1, source_target_pairs={{0,4},{1,5},{2,6},{3,7},{4,0},{5,1},{6,2},{7,3},{8,12},{9,13},{10,... | collective-permute-start | bytes 6144008 | tf_op jit(solution)/shard_map/ppermute | solution.py:14
  145.4 1.6 copy-start.3
  145.5 242.5 %all-reduce.6.cloned.1.call-start = ((), (), s32[]{:S(2)}) async-start(), calls=%async_computation.1 | async-start | bytes 262144
  218.6 1.6 copy-start.1
  229.1 159.6 %copy-start = (f32[512,1024]{1,0:T(8,128)S(1)}, f32[512,1024]{1,0:T(8,128)}, u32[]{:S(2)}) copy-start(f32[512,1024]{1,0:T(8,128)} %param.11) | copy-start | bytes 6291460
  1251.8 0.6 copy-start.6
Sparse Core Ops, SparseCore 0:
  145.6 71.4 all-reduce.3
  265.1 122.8 all-reduce.5
